TPU v7x, 32 devices: a whole 2x2x4 slice. The times are simulated.
32 devices in a mesh: row: 4 (over x, core), col: 8 (over z, y).
Axes of the slice: x: 2, y: 2, z: 4, core: 2. Of those that a mesh axis runs over, the one named last changes fastest.
Arguments:
- pair: bfloat16 [768, 768, 512], P('row', 'col'), may hold values from -6 to 6
- w_bias: bfloat16 [512, 96], replicated, may hold values from -0.25 to 0.25
- queries: bfloat16 [768, 1536], P('row', 'col'), may hold values from -360 to 360
- keys: bfloat16 [768, 1536], P('col', 'row'), may hold values from -6 to 6
- values: bfloat16 [768, 1536], P('col', 'row'), may hold values from -6 to 6
- d_out: bfloat16 [768, 1536], P('row', 'col'), may hold values from -6 to 6
Outputs:
- d_pair: bfloat16 [768, 768, 512], P('row', 'col')
- d_wbias: float32 [512, 96], replicated
- d_queries: bfloat16 [768, 1536], P('row', 'col')
- d_keys: bfloat16 [768, 1536], P('col', 'row')
- d_values: bfloat16 [768, 1536], P('col', 'row')
All inputs are finite; a program needn't handle non-finite values.
Results may differ from a plain program's by a relative error of at most 0.0095.
Values may be sent and summed in bfloat16 or wider, within the bound.
A program may use at most 128 MiB of HBM per device.

v0:
```python
import jax
import jax.numpy as jnp
from jax import lax
from jax.sharding import PartitionSpec as P

D = 1536
H = 96
P_SIZE = 512
HD = 16


def joined(value, axis, join):
    pieces = jax.tree.map(lambda part: lax.all_gather(part, axis), value)
    head = jax.tree.map(lambda part: part[0], pieces)
    tail = jax.tree.map(lambda part: part[1:], pieces)
    subtotal, _ = lax.scan(lambda subtotal, piece: (join(subtotal, piece), None), head, tail)
    return subtotal


def combine_stats(former, latter):
    joined_max = jnp.maximum(former[0], latter[0])
    scale_former = jnp.exp(former[0] - joined_max)
    scale_latter = jnp.exp(latter[0] - joined_max)
    return (
        joined_max,
        former[1] * scale_former + latter[1] * scale_latter,
        former[2] * scale_former + latter[2] * scale_latter,
    )


def on_device(pair, w_bias, queries, keys, values, d_out):
    row_count = pair.shape[0]
    col_count = pair.shape[1]
    query_full, out_full = (
        lax.all_gather(queries, "col", axis=1, tiled=True),
        lax.all_gather(d_out, "col", axis=1, tiled=True),
    )
    key_full, value_full = (
        lax.all_gather(keys, "row", axis=1, tiled=True),
        lax.all_gather(values, "row", axis=1, tiled=True),
    )
    query_heads = query_full.reshape(row_count, H, HD)
    out_heads = out_full.reshape(row_count, H, HD)
    key_heads = key_full.reshape(col_count, H, HD)
    value_heads = value_full.reshape(col_count, H, HD)
    flat_pair = pair.reshape(row_count * col_count, P_SIZE)
    pair_bias = jnp.dot(flat_pair, w_bias, preferred_element_type=jnp.float32).reshape(
        row_count, col_count, H
    )
    scale = 1.0 / HD**0.5
    scores = jnp.einsum(
        "ihd,jhd->hij", query_heads, key_heads, preferred_element_type=jnp.float32
    ) * scale + pair_bias.transpose(2, 0, 1)
    grad_prob = jnp.einsum(
        "ihd,jhd->hij", out_heads, value_heads, preferred_element_type=jnp.float32
    )
    local_max = jnp.max(scores, axis=-1)
    exp_scores = jnp.exp(scores - local_max[..., None])
    local_stats = (
        local_max,
        jnp.sum(exp_scores, axis=-1),
        jnp.sum(exp_scores * grad_prob, axis=-1),
    )
    row_max, row_total, row_upper = joined(local_stats, "col", combine_stats)
    weights = jnp.exp(scores - row_max[..., None]) / row_total[..., None]
    row_delta = row_upper / row_total
    grad_score = (weights * (grad_prob - row_delta[..., None])).astype(jnp.bfloat16)
    weights_low = weights.astype(jnp.bfloat16)
    score_flat = grad_score.transpose(1, 2, 0).reshape(row_count * col_count, H)
    d_pair = (
        jnp.dot(score_flat, w_bias.T, preferred_element_type=jnp.float32)
        .astype(jnp.bfloat16)
        .reshape(row_count, col_count, P_SIZE)
    )
    weight_term = jnp.dot(flat_pair.T, score_flat, preferred_element_type=jnp.float32)
    d_wbias = lax.psum(weight_term, ("row", "col"))
    query_term = (
        jnp.einsum("hij,jhd->ihd", grad_score, key_heads, preferred_element_type=jnp.float32)
        * scale
    ).reshape(row_count, D)
    key_term = (
        jnp.einsum("hij,ihd->jhd", grad_score, query_heads, preferred_element_type=jnp.float32)
        * scale
    ).reshape(col_count, D)
    value_term = jnp.einsum(
        "hij,ihd->jhd", weights_low, out_heads, preferred_element_type=jnp.float32
    ).reshape(col_count, D)
    query_grad = lax.psum_scatter(query_term, "col", scatter_dimension=1, tiled=True)
    key_grad, value_grad = (
        lax.psum_scatter(key_term, "row", scatter_dimension=1, tiled=True),
        lax.psum_scatter(value_term, "row", scatter_dimension=1, tiled=True),
    )
    return (
        d_pair,
        d_wbias,
        query_grad.astype(jnp.bfloat16),
        key_grad.astype(jnp.bfloat16),
        value_grad.astype(jnp.bfloat16),
    )


def solution(mesh):
    return jax.shard_map(
        on_device,
        mesh=mesh,
        in_specs=(
            P("row", "col", None),
            P(),
            P("row", "col"),
            P("col", "row"),
            P("col", "row"),
            P("row", "col"),
        ),
        out_specs=(P("row", "col", None), P(), P("row", "col"), P("col", "row"), P("col", "row")),
        check_vma=False,
    )
```

profile of v0, /device:TPU:8, one launch (start us, length us, event | category | flops | bytes accessed | tf_op | source)
XLA Modules:
  0.0 433.7 jit_solution(17199849973470065205)
XLA Ops:
  8.9 11.2 %fusion.11 = f32[192,96,96]{2,1,0:T(8,128)} fusion(bf16[192,96,512]{2,1,0:T(8,128)(2,1)} %param.8, bf16[512,96]{0,1:T(8,128)(2,1)S(1)} %copy-done), kind=kOutput, calls=%fused_computation.27 | convolution fusion | flops 1811939328 | bytes 26050560 | tf_op jit(solution)/shard_map/dot_general | solution.py:47
  20.1 12.1 %copy.40 = f32[192,96,96]{0,1,2:T(8,128)} copy(f32[192,96,96]{2,1,0:T(8,128)} %fusion.11) | data formatting | bytes 14155776 | tf_op jit(solution)/shard_map/dot_general | solution.py:47
  32.4 29.7 %all_gather.30 = bf16[192,1536]{0,1:T(8,128)(2,1)S(1)} all-gather(bf16[192,192]{0,1:T(8,128)(2,1)S(1)} %copy.38), channel_id=1, replica_groups=mesh['row'=4,'col'=8] {'col'}, dimensions={1}, use_global_device_ids=true | all-gather | bytes 663552 | tf_op jit(solution)/shard_map/all_gather | solution.py:35
  62.1 5.9 %all_gather.31 = bf16[96,1536]{1,0:T(8,128)(2,1)S(1)} all-gather(bf16[96,384]{1,0:T(8,128)(2,1)S(1)} %copy-done.5), channel_id=1, replica_groups=mesh['row'=4,'col'=8] {'row'}, dimensions={1}, use_global_device_ids=true | all-gather | bytes 368640 | tf_op jit(solution)/shard_map/all_gather | solution.py:39
  68.4 32.2 %all_gather.36 = bf16[192,1536]{0,1:T(8,128)(2,1)S(1)} all-gather(bf16[192,192]{0,1:T(8,128)(2,1)S(1)} %copy.42), channel_id=1, replica_groups=mesh['row'=4,'col'=8] {'col'}, dimensions={1}, use_global_device_ids=true | all-gather | bytes 663552 | tf_op jit(solution)/shard_map/all_gather | solution.py:36
  100.6 5.9 %all_gather.37 = bf16[96,1536]{1,0:T(8,128)(2,1)S(1)} all-gather(bf16[96,384]{1,0:T(8,128)(2,1)S(1)} %copy-done.6), channel_id=1, replica_groups=mesh['row'=4,'col'=8] {'row'}, dimensions={1}, use_global_device_ids=true | all-gather | bytes 368640 | tf_op jit(solution)/shard_map/all_gather | solution.py:40
  106.7 9.2 %fusion.13 = (f32[96,192]{1,0:T(8,128)S(1)}, f32[96,192,96]{1,2,0:T(8,128)S(1)}, f32[96,192,96]{1,2,0:T(8,128)}) fusion(f32[192,96,96]{0,1,2:T(8,128)} %copy.40, bf16[192,96,16]{0,2,1:T(8,128)(2,1)S(1)} %bitcast.92, bf16[96,96,16]{0,2,1:T(8,128)(2,1)S(1)} %bitcast.96), kind=kOutput, calls=%fused_computation.29 | convolution fusion | flops 61913088 | bytes 22192128 | tf_op jit(solution)/shard_map/ihd,jhd->hij/dot_general | solution.py:51
  115.8 5.7 %multiply_reduce_fusion = (f32[96,192]{1,0:T(8,128)S(1)}, f32[96,192]{1,0:T(8,128)S(1)}, f32[96,192,96]{1,2,0:T(8,128)}) fusion(f32[96,192,96]{1,2,0:T(8,128)S(1)} %get-tuple-element.66, f32[96,192]{1,0:T(8,128)S(1)} %get-tuple-element.65, bf16[192,96,16]{0,2,1:T(8,128)(2,1)S(1)} %bitcast.98, bf16[96,96,16]{0,2,1:T(8,128)(2,1)S(1)} %bitcast.103), kind=kOutput, calls=%fused_computation.19 | convolution fusion | flops 63664128 | bytes 15261696 | tf_op jit(solution)/shard_map/ihd,jhd->hij/dot_general | solution.py:54
  122.1 32.1 %all-gather.1 = f32[768,192]{1,0:T(8,128)S(1)} all-gather(f32[96,192]{1,0:T(8,128)S(1)} %get-tuple-element.48), channel_id=3, replica_groups=mesh['row'=4,'col'=8] {'col'}, dimensions={0}, use_global_device_ids=true | all-gather | bytes 663552 | tf_op jit(solution)/shard_map/all_gather | solution.py:13
  155.2 32.1 %all-gather.2 = f32[768,192]{1,0:T(8,128)S(1)} all-gather(f32[96,192]{1,0:T(8,128)S(1)} %get-tuple-element.47), channel_id=4, replica_groups=mesh['row'=4,'col'=8] {'col'}, dimensions={0}, use_global_device_ids=true | all-gather | bytes 663552 | tf_op jit(solution)/shard_map/all_gather | solution.py:13
  188.2 32.0 %all-gather = f32[768,192]{1,0:T(8,128)S(1)} all-gather(f32[96,192]{1,0:T(8,128)S(1)} %get-tuple-element.65), channel_id=2, replica_groups=mesh['row'=4,'col'=8] {'col'}, dimensions={0}, use_global_device_ids=true | all-gather | bytes 663552 | tf_op jit(solution)/shard_map/all_gather | solution.py:13
  220.3 13.8 %while.14 = (s32[]{:T(128)}, f32[96,192]{1,0:T(8,128)S(1)}, f32[96,192]{1,0:T(8,128)S(1)}, f32[96,192]{1,0:T(8,128)S(1)}, f32[7,96,192]{2,1,0:T(8,128)S(1)}, /*i...) while((s32[]{:T(128)}, f32[96,192]{1,0:T(8,128)S(1)}, f32[96,192]{1,0:T(8,128)S(1)}, ...), condition=%wide.region_4.5_spmd, body=%wide.region_3.4_spmd.sunk | while | flops 202754 | bytes 1032285 | solution.py:16
  234.2 6.2 %fusion.9 = f32[96,96,16]{1,2,0:T(8,128)} fusion(bf16[192,96,16]{0,2,1:T(8,128)(2,1)S(1)} %bitcast.99, f32[96,192,96]{1,2,0:T(8,128)} %copy-done.1, f32[96,192]{1,0:T(8,128)S(1)} %get-tuple-element.45, f32[96,192]{1,0:T(8,128)S(1)} %get-tuple-element.44), kind=kOutput, calls=%fused_computation.22 | convolution fusion | flops 61931520 | bytes 8404992 | tf_op jit(solution)/shard_map/hij,ihd->jhd/dot_general | solution.py:85
  240.3 2.2 copy.51
  242.8 7.9 %multiply_convert_fusion = bf16[96,192,96]{1,2,0:T(8,128)(2,1)S(1)} fusion(f32[96,192,96]{1,2,0:T(8,128)} %get-tuple-element.68, f32[96,192]{1,0:T(8,128)S(1)} %div.21, f32[96,192]{1,0:T(8,128)S(1)} %get-tuple-element.45, f32[96,192,96]{1,2,0:T(8,128)} %copy-done.1, f32[96,192]{1,0:T(8,128)S(1)} %get-tuple-element.44), kind=kLoop, calls=%fused_computation.17 | loop fusion | flops 8847360 | bytes 17915904 | tf_op jit(solution)/shard_map/convert_element_type | solution.py:67
  255.4 4.2 convolution_multiply_fusion
  259.7 13.1 %fusion.4 = bf16[192,96,96]{0,1,2:T(8,128)(2,1)} fusion(f32[96,192,96]{1,2,0:T(8,128)} %get-tuple-element.68, f32[192,96,96]{0,1,2:T(8,128)} %copy.40, f32[96,192,96]{1,2,0:T(8,128)} %get-tuple-element.67, f32[192,96]{0,1:T(8,128)S(1)} %bitcast.104, f32[192,96]{0,1:T(8,128)S(1)} %bitcast.91, f32[192,96]{0,1:T(8,128)S(1)} %bitcast.90), kind=kLoop, calls=%fused_computation.11 | loop fusion | flops 12386304 | bytes 24993792 | tf_op jit(solution)/shard_map/convert_element_type | solution.py:67
  272.8 7.6 %copy.45 = bf16[192,96,96]{1,2,0:T(8,128)(2,1)} copy(bf16[192,96,96]{0,1,2:T(8,128)(2,1)} %fusion.4) | data formatting | bytes 7077888 | tf_op jit(solution)/shard_map/convert_element_type | solution.py:67
  280.5 11.8 %convolution_bitcast_fusion = f32[512,96]{0,1:T(8,128)} fusion(bf16[192,96,96]{1,2,0:T(8,128)(2,1)} %copy.45, bf16[192,96,512]{2,1,0:T(8,128)(2,1)} %param.8), kind=kOutput, calls=%fused_computation.26 | convolution fusion | flops 1811939328 | bytes 22609920 | tf_op jit(solution)/shard_map/dot_general | solution.py:75
  292.2 6.7 %copy.44 = bf16[192,96,96]{1,0,2:T(8,128)(2,1)} copy(bf16[192,96,96]{0,1,2:T(8,128)(2,1)} %fusion.4) | data formatting | bytes 7077888 | tf_op jit(solution)/shard_map/convert_element_type | solution.py:67
  299.0 9.2 %reshape.49 = bf16[18432,96]{0,1:T(8,128)(2,1)} reshape(bf16[192,96,96]{1,0,2:T(8,128)(2,1)} %copy.44) | data formatting | bytes 7077888 | tf_op jit(solution)/shard_map/reshape | solution.py:69
  308.2 11.5 %convolution_convert_fusion = bf16[18432,512]{1,0:T(8,128)(2,1)} fusion(bf16[18432,96]{0,1:T(8,128)(2,1)} %reshape.49, bf16[512,96]{0,1:T(8,128)(2,1)S(1)} %copy-done), kind=kOutput, calls=%fused_computation.8 | convolution fusion | flops 1821376512 | bytes 22511616 | tf_op jit(solution)/shard_map/dot_general | solution.py:71
  322.8 38.5 %reduce-scatter.10.cloned.1.call-done = f32[192,192]{1,0:T(8,128)} async-done(((f32[1536,192]{1,0:T(8,128)}), f32[192,192]{1,0:T(8,128)}) %reduce-scatter.10.cloned.1.call-update) | async-done | bytes 147472
  363.0 61.9 %all-reduce.2.cloned.1.call-done = f32[512,96]{0,1:T(8,128)} async-done(((f32[512,96]{0,1:T(8,128)}), f32[512,96]{0,1:T(8,128)}) %all-reduce.2.cloned.1.call-update) | async-done | bytes 196624 | tf_op jit(solution)/shard_map/psum | solution.py:76
  (62 shorter events, 29.1 us)
Async XLA Ops:
  8.0 0.9 copy-start
  8.0 311.7 %reduce-scatter.8.cloned.1.call-start = ((), (), s32[]{:S(2)}) async-start(), calls=%async_computation.5 | async-start | bytes 737280 | tf_op jit(solution)/shard_map/reduce_scatter | solution.py:91
  20.1 12.2 %copy-start.3 = (bf16[192,192]{1,0:T(8,128)(2,1)S(1)}, bf16[192,192]{1,0:T(8,128)(2,1)}, u32[]{:S(2)}) copy-start(bf16[192,192]{1,0:T(8,128)(2,1)} %param.10) | copy-start | bytes 221188
  20.1 42.0 %copy-start.5 = (bf16[96,384]{1,0:T(8,128)(2,1)S(1)}, bf16[96,384]{1,0:T(8,128)(2,1)}, u32[]{:S(2)}) copy-start(bf16[96,384]{1,0:T(8,128)(2,1)} %param.11) | copy-start | bytes 221188
  20.1 48.1 %copy-start.4 = (bf16[192,192]{1,0:T(8,128)(2,1)S(1)}, bf16[192,192]{1,0:T(8,128)(2,1)}, u32[]{:S(2)}) copy-start(bf16[192,192]{1,0:T(8,128)(2,1)} %param.13) | copy-start | bytes 221188
  20.1 80.5 %copy-start.6 = (bf16[96,384]{1,0:T(8,128)(2,1)S(1)}, bf16[96,384]{1,0:T(8,128)(2,1)}, u32[]{:S(2)}) copy-start(bf16[96,384]{1,0:T(8,128)(2,1)} %param.12) | copy-start | bytes 221188
  115.8 6.3 %copy-start.1 = (f32[96,192,96]{1,2,0:T(8,128)}, f32[96,192,96]{1,2,0:T(8,128)S(1)}, u32[]{:S(2)}) copy-start(f32[96,192,96]{1,2,0:T(8,128)S(1)} %get-tuple-element.66) | copy-start | bytes 21233668
  242.6 78.7 %reduce-scatter.6.cloned.1.call-start = ((), (), s32[]{:S(2)}) async-start(), calls=%async_computation.4 | async-start | bytes 737280 | tf_op jit(solution)/shard_map/reduce_scatter | solution.py:90
  250.7 2.2 copy-start.2
  255.4 106.0 %reduce-scatter.10.cloned.1.call-start = ((), (), s32[]{:S(2)}) async-start(), calls=%async_computation.6 | async-start | bytes 1769472
  259.7 165.3 %all-reduce.2.cloned.1.call-start = ((), (), s32[]{:S(2)}) async-start(), calls=%async_computation.3 | async-start | bytes 393216 | tf_op jit(solution)/shard_map/psum | solution.py:76
Sparse Core Ops, SparseCore 0:
  242.7 25.4 reduce-scatter.7
  270.7 22.0 reduce-scatter.5
  296.2 65.0 reduce-scatter.9
Sparse Core Ops, SparseCore 1:
  292.3 132.6 all-reduce.1
where the time goes:
time: 435 us; the launch traced here: 434 us
  blocking collectives  170 us (39%)
  waiting for transfers between devices  101 us (23%)
  matrix products  61.1 us (14%)
  local copies, waits for them, and re-layouts  48.6 us (11%)
  other arithmetic  37.7 us (9%)
  between operations  15.3 us (4%)
    all_gather x3, blocking collectives, joined(): pieces = jax.tree.map(lambda part: lax.all_gather(part, axis), value)  96.3 us
    psum x1, waiting for transfers between devices, on_device(): d_wbias = lax.psum(weight_term, ('row', 'col'))  61.9 us
    unnamed x5, waiting for transfers between devices  38.6 us
    all_gather x1, blocking collectives, on_device(): lax.all_gather(d_out, 'col', axis=1, tiled=True)  32.2 us
    all_gather x1, blocking collectives, on_device(): lax.all_gather(queries, 'col', axis=1, tiled=True)  29.7 us
    convert_element_type x2, other arithmetic, on_device(): (weights * (grad_prob - row_delta[..., None])).astype(jnp.bfloat16)  21 us
    convert_element_type x2, local copies, waits for them, and re-layouts, on_device(): (weights * (grad_prob - row_delta[..., None])).astype(jnp.bfloat16)  14.4 us
    dot_general x1, local copies, waits for them, and re-layouts, on_device(): jnp.dot(flat_pair, w_bias, preferred_element_type=jnp.float32)  12.1 us
  transfers between devices with their start and end apart: 4, of which 2 were waited for; matrix products, arithmetic and copies ran while one was open for 18% of the time, Pallas kernels for 0%

commit v1 on v0

--- a/solution.py
+++ b/solution.py
@@ -1,3 +1,4 @@
+import functools
 import jax
 import jax.numpy as jnp
 from jax import lax
@@ -7,6 +8,27 @@
 H = 96
 P_SIZE = 512
 HD = 16
+
+
+def serve_entries(local_x, axis_no):
+    h_now, far_arr, t1 = (
+        jax.lax.axis_size("col"),
+        jax.lax.axis_index("col"),
+        local_x.shape[axis_no],
+    )
+    runs = [i * h_now if m == axis_no else i for m, i in enumerate(local_x.shape)]
+    frame_out = lax.dynamic_update_slice_in_dim(
+        jnp.zeros(runs, local_x.dtype), local_x, far_arr * t1, axis=axis_no
+    )
+    for t in range(1, h_now):
+        local_x = jax.lax.ppermute(local_x, "col", [(m, (m + 1) % h_now) for m in range(h_now)])
+        frame_out = lax.dynamic_update_slice_in_dim(
+            frame_out, local_x, (far_arr - t) % h_now * t1, axis=axis_no
+        )
+    return frame_out
+
+
+_define_map = functools.partial(serve_entries, axis_no=1)
 
 
 def joined(value, axis, join):
@@ -31,10 +53,7 @@
 def on_device(pair, w_bias, queries, keys, values, d_out):
     row_count = pair.shape[0]
     col_count = pair.shape[1]
-    query_full, out_full = (
-        lax.all_gather(queries, "col", axis=1, tiled=True),
-        lax.all_gather(d_out, "col", axis=1, tiled=True),
-    )
+    query_full, out_full = (lax.all_gather(queries, "col", axis=1, tiled=True), _define_map(d_out))
     key_full, value_full = (
         lax.all_gather(keys, "row", axis=1, tiled=True),
         lax.all_gather(values, "row", axis=1, tiled=True),

time: 435 us -> 470 us (1.080)
  waiting for transfers between devices: 101 us -> 151 us
  blocking collectives: 170 us -> 143 us
  matrix products: 61.1 us -> 66.2 us
    ppermute x0 -> x7, waiting for transfers between devices: none -> 40.3 us  [serve_entries(): jax.lax.ppermute(local_x, 'col', [(m, (m + 1) % h_now) for m in range(h_n...]
    all_gather x1 -> x0, blocking collectives: 32.2 us -> none  [on_device(): lax.all_gather(d_out, 'col', axis=1, tiled=True)]
    psum x1, waiting for transfers between devices: 61.9 us -> 76.3 us  [on_device(): d_wbias = lax.psum(weight_term, ('row', 'col'))]
    all_gather x3, blocking collectives: 96.3 us -> 102 us  [joined(): pieces = jax.tree.map(lambda part: lax.all_gather(part, axis), value)]
  transfers between devices with their start and end apart: 4 -> 11, of which waited for: 2 -> 8; matrix products, arithmetic and copies ran while one was open for 18% -> 25% of each run, Pallas kernels for 0% -> 0%
where the time goes in v1:
time: 470 us; the launch traced here: 469 us
  waiting for transfers between devices  151 us (32%)
  blocking collectives  143 us (30%)
  matrix products  66.2 us (14%)
  local copies, waits for them, and re-layouts  52.6 us (11%)
  other arithmetic  37.7 us (8%)
  between operations  15.7 us (3%)
    all_gather x3, blocking collectives, joined(): pieces = jax.tree.map(lambda part: lax.all_gather(part, axis), value)  102 us
    psum x1, waiting for transfers between devices, on_device(): d_wbias = lax.psum(weight_term, ('row', 'col'))  76.3 us
    ppermute x7, waiting for transfers between devices, serve_entries(): jax.lax.ppermute(local_x, 'col', [(m, (m + 1) % h_now) for m in range(h_n...  40.3 us
    unnamed x5, waiting for transfers between devices  34.6 us
    all_gather x1, blocking collectives, on_device(): lax.all_gather(queries, 'col', axis=1, tiled=True)  29.7 us
    convert_element_type x2, other arithmetic, on_device(): (weights * (grad_prob - row_delta[..., None])).astype(jnp.bfloat16)  20.9 us
    convert_element_type x2, local copies, waits for them, and re-layouts, on_device(): (weights * (grad_prob - row_delta[..., None])).astype(jnp.bfloat16)  14.5 us
    dot_general x1, matrix products, on_device(): jnp.einsum('ihd,jhd->hij', query_heads, key_heads, preferred_element_type...  12.3 us
  transfers between devices with their start and end apart: 11, of which 8 were waited for; matrix products, arithmetic and copies ran while one was open for 25% of the time, Pallas kernels for 0%

profile of v1, /device:TPU:8, one launch (start us, length us, event | category | flops | bytes accessed | tf_op | source)
XLA Modules:
  0.0 468.6 jit_solution(5849390353040049422)
XLA Ops:
  10.8 11.2 %fusion.11 = f32[192,96,96]{2,1,0:T(8,128)} fusion(bf16[192,96,512]{2,1,0:T(8,128)(2,1)} %param.8, bf16[512,96]{0,1:T(8,128)(2,1)S(1)} %copy-done), kind=kOutput, calls=%fused_computation.27 | convolution fusion | flops 1811939328 | bytes 26050560 | tf_op jit(solution)/shard_map/dot_general | solution.py:66
  22.0 12.1 %copy.54 = f32[192,96,96]{0,1,2:T(8,128)} copy(f32[192,96,96]{2,1,0:T(8,128)} %fusion.11) | data formatting | bytes 14155776 | tf_op jit(solution)/shard_map/dot_general | solution.py:66
  34.2 29.7 %all_gather.27 = bf16[192,1536]{0,1:T(8,128)(2,1)S(1)} all-gather(bf16[192,192]{0,1:T(8,128)(2,1)S(1)} %copy.52), channel_id=1, replica_groups=mesh['row'=4,'col'=8] {'col'}, dimensions={1}, use_global_device_ids=true | all-gather | bytes 663552 | tf_op jit(solution)/shard_map/all_gather | solution.py:56
  70.1 12.3 %fusion.13 = (f32[96,192]{1,0:T(8,128)S(1)}, f32[96,192,96]{1,2,0:T(8,128)}, f32[96,192,96]{1,2,0:T(8,128)}) fusion(f32[192,96,96]{0,1,2:T(8,128)} %copy.54, bf16[192,96,16]{0,2,1:T(8,128)(2,1)S(1)} %bitcast.92, bf16[96,96,16]{0,2,1:T(8,128)(2,1)S(1)} %bitcast.96), kind=kOutput, calls=%fused_computation.37 | convolution fusion | flops 61913088 | bytes 22192128 | tf_op jit(solution)/shard_map/ihd,jhd->hij/dot_general | solution.py:70
  82.4 32.3 %all-gather = f32[768,192]{1,0:T(8,128)S(1)} all-gather(f32[96,192]{1,0:T(8,128)S(1)} %get-tuple-element.65), channel_id=2, replica_groups=mesh['row'=4,'col'=8] {'col'}, dimensions={0}, use_global_device_ids=true | all-gather | bytes 663552 | tf_op jit(solution)/shard_map/all_gather | solution.py:35
  122.0 6.1 %collective-permute-done.1 = bf16[192,192]{1,0:T(8,128)(2,1)S(1)} collective-permute-done((bf16[192,192]{1,0:T(8,128)(2,1)}, bf16[192,192]{1,0:T(8,128)(2,1)S(1)}, u32[]{:S(2)}, u32[]{:S(2)}) %collective-permute-start.1) | collective-permute-done | bytes 73760 | tf_op jit(solution)/shard_map/ppermute | solution.py:24
  135.0 6.4 %collective-permute-done.3 = bf16[192,192]{1,0:T(8,128)(2,1)S(1)} collective-permute-done((bf16[192,192]{1,0:T(8,128)(2,1)}, bf16[192,192]{1,0:T(8,128)(2,1)S(1)}, u32[]{:S(2)}, u32[]{:S(2)}) %collective-permute-start.3) | collective-permute-done | bytes 73760 | tf_op jit(solution)/shard_map/ppermute | solution.py:24
  141.6 7.4 %collective-permute-done.4 = bf16[192,192]{1,0:T(8,128)(2,1)} collective-permute-done((bf16[192,192]{1,0:T(8,128)(2,1)S(1)}, bf16[192,192]{1,0:T(8,128)(2,1)}, u32[]{:S(2)}, u32[]{:S(2)}) %collective-permute-start.4) | collective-permute-done | bytes 73760 | tf_op jit(solution)/shard_map/ppermute | solution.py:24
  150.0 7.5 %collective-permute-done.5 = bf16[192,192]{1,0:T(8,128)(2,1)S(1)} collective-permute-done((bf16[192,192]{1,0:T(8,128)(2,1)}, bf16[192,192]{1,0:T(8,128)(2,1)S(1)}, u32[]{:S(2)}, u32[]{:S(2)}) %collective-permute-start.5) | collective-permute-done | bytes 73760 | tf_op jit(solution)/shard_map/ppermute | solution.py:24
  157.7 7.4 %collective-permute-done.6 = bf16[192,192]{1,0:T(8,128)(2,1)} collective-permute-done((bf16[192,192]{1,0:T(8,128)(2,1)S(1)}, bf16[192,192]{1,0:T(8,128)(2,1)}, u32[]{:S(2)}, u32[]{:S(2)}) %collective-permute-start.6) | collective-permute-done | bytes 73760 | tf_op jit(solution)/shard_map/ppermute | solution.py:24
  166.1 7.6 %multiply_reduce_fusion = (f32[96,192]{1,0:T(8,128)S(1)}, f32[96,192]{1,0:T(8,128)S(1)}, f32[96,192,96]{1,2,0:T(8,128)}) fusion(f32[96,192,96]{1,2,0:T(8,128)} %get-tuple-element.66, f32[96,192]{1,0:T(8,128)S(1)} %get-tuple-element.65, bf16[192,96,16]{0,2,1:T(8,128)(2,1)S(1)} %bitcast.98, bf16[96,96,16]{0,2,1:T(8,128)(2,1)S(1)} %bitcast.103), kind=kOutput, calls=%fused_computation.19 | convolution fusion | flops 63664128 | bytes 15261696 | tf_op jit(solution)/shard_map/ihd,jhd->hij/dot_general | solution.py:73
  173.7 37.3 %all-gather.1 = f32[768,192]{1,0:T(8,128)S(1)} all-gather(f32[96,192]{1,0:T(8,128)S(1)} %get-tuple-element.48), channel_id=3, replica_groups=mesh['row'=4,'col'=8] {'col'}, dimensions={0}, use_global_device_ids=true | all-gather | bytes 663552 | tf_op jit(solution)/shard_map/all_gather | solution.py:35
  211.9 31.9 %all-gather.2 = f32[768,192]{1,0:T(8,128)S(1)} all-gather(f32[96,192]{1,0:T(8,128)S(1)} %get-tuple-element.47), channel_id=4, replica_groups=mesh['row'=4,'col'=8] {'col'}, dimensions={0}, use_global_device_ids=true | all-gather | bytes 663552 | tf_op jit(solution)/shard_map/all_gather | solution.py:35
  244.8 13.8 %while.14 = (s32[]{:T(128)}, f32[96,192]{1,0:T(8,128)S(1)}, f32[96,192]{1,0:T(8,128)S(1)}, f32[96,192]{1,0:T(8,128)S(1)}, f32[7,96,192]{2,1,0:T(8,128)S(1)}, /*i...) while((s32[]{:T(128)}, f32[96,192]{1,0:T(8,128)S(1)}, f32[96,192]{1,0:T(8,128)S(1)}, ...), condition=%wide.region_4.5_spmd, body=%wide.region_3.4_spmd.sunk | while | flops 202754 | bytes 1032285 | solution.py:38
  258.6 6.1 %fusion.9 = f32[96,16,96]{2,1,0:T(8,128)} fusion(bf16[192,96,16]{0,2,1:T(8,128)(2,1)S(1)} %bitcast.99, f32[96,192,96]{1,2,0:T(8,128)} %get-tuple-element.66, f32[96,192]{1,0:T(8,128)S(1)} %get-tuple-element.45, f32[96,192]{1,0:T(8,128)S(1)} %get-tuple-element.44), kind=kOutput, calls=%fused_computation.22 | convolution fusion | flops 61931520 | bytes 8404992 | tf_op jit(solution)/shard_map/hij,ihd->jhd/dot_general | solution.py:104
  267.1 8.0 %multiply_convert_fusion = bf16[96,192,96]{1,2,0:T(8,128)(2,1)S(1)} fusion(f32[96,192,96]{1,2,0:T(8,128)} %get-tuple-element.68, f32[96,192]{1,0:T(8,128)S(1)} %div.21, f32[96,192]{1,0:T(8,128)S(1)} %get-tuple-element.45, f32[96,192,96]{1,2,0:T(8,128)} %get-tuple-element.66, f32[96,192]{1,0:T(8,128)S(1)} %get-tuple-element.44), kind=kLoop, calls=%fused_computation.17 | loop fusion | flops 8847360 | bytes 17915904 | tf_op jit(solution)/shard_map/convert_element_type | solution.py:86
  284.1 12.9 %fusion.4 = bf16[192,96,96]{0,1,2:T(8,128)(2,1)} fusion(f32[96,192,96]{1,2,0:T(8,128)} %get-tuple-element.68, f32[192,96,96]{0,1,2:T(8,128)} %copy.54, f32[96,192,96]{1,2,0:T(8,128)} %get-tuple-element.67, f32[192,96]{0,1:T(8,128)S(1)} %bitcast.104, f32[192,96]{0,1:T(8,128)S(1)} %bitcast.91, f32[192,96]{0,1:T(8,128)S(1)} %bitcast.90), kind=kLoop, calls=%fused_computation.11 | loop fusion | flops 12386304 | bytes 24993792 | tf_op jit(solution)/shard_map/convert_element_type | solution.py:86
  297.1 6.8 %copy.65 = bf16[192,96,96]{1,0,2:T(8,128)(2,1)} copy(bf16[192,96,96]{0,1,2:T(8,128)(2,1)} %fusion.4) | data formatting | bytes 7077888 | tf_op jit(solution)/shard_map/convert_element_type | solution.py:86
  303.9 7.7 %copy.66 = bf16[192,96,96]{1,2,0:T(8,128)(2,1)} copy(bf16[192,96,96]{0,1,2:T(8,128)(2,1)} %fusion.4) | data formatting | bytes 7077888 | tf_op jit(solution)/shard_map/convert_element_type | solution.py:86
  311.6 9.2 %reshape.49 = bf16[18432,96]{0,1:T(8,128)(2,1)} reshape(bf16[192,96,96]{1,0,2:T(8,128)(2,1)} %copy.65) | data formatting | bytes 7077888 | tf_op jit(solution)/shard_map/reshape | solution.py:88
  320.8 11.8 %convolution_bitcast_fusion = f32[512,96]{0,1:T(8,128)} fusion(bf16[192,96,96]{1,2,0:T(8,128)(2,1)} %copy.66, bf16[192,96,512]{2,1,0:T(8,128)(2,1)} %param.8), kind=kOutput, calls=%fused_computation.26 | convolution fusion | flops 1811939328 | bytes 22609920 | tf_op jit(solution)/shard_map/dot_general | solution.py:94
  332.6 11.6 %convolution_convert_fusion = bf16[18432,512]{1,0:T(8,128)(2,1)} fusion(bf16[18432,96]{0,1:T(8,128)(2,1)} %reshape.49, bf16[512,96]{0,1:T(8,128)(2,1)S(1)} %copy-done), kind=kOutput, calls=%fused_computation.8 | convolution fusion | flops 1821376512 | bytes 22511616 | tf_op jit(solution)/shard_map/dot_general | solution.py:90
  347.3 34.5 %reduce-scatter.10.cloned.1.call-done = f32[192,192]{1,0:T(8,128)} async-done(((f32[1536,192]{1,0:T(8,128)}), f32[192,192]{1,0:T(8,128)}) %reduce-scatter.10.cloned.1.call-update) | async-done | bytes 147472
  383.5 76.3 %all-reduce.2.cloned.1.call-done = f32[512,96]{0,1:T(8,128)} async-done(((f32[512,96]{0,1:T(8,128)}), f32[512,96]{0,1:T(8,128)}) %all-reduce.2.cloned.1.call-update) | async-done | bytes 196624 | tf_op jit(solution)/shard_map/psum | solution.py:95
  (87 shorter events, 58.7 us)
Async XLA Ops:
  8.0 2.8 copy-start
  8.0 336.2 %reduce-scatter.8.cloned.1.call-start = ((), (), s32[]{:S(2)}) async-start(), calls=%async_computation.5 | async-start | bytes 737280 | tf_op jit(solution)/shard_map/reduce_scatter | solution.py:110
  8.1 112.9 %collective-permute-start = (bf16[192,192]{1,0:T(8,128)(2,1)}, bf16[192,192]{1,0:T(8,128)(2,1)}, u32[]{:S(2)}, u32[]{:S(2)}) collective-permute-start(bf16[192,192]{1,0:T(8,128)(2,1)} %param.13), channel_id=1, source_target_pairs={{0,1},{1,2},{2,3},{3,4},{4,5},{5,6},{6,7},{7,0},{8,9},{9,10},{10,1... | collective-permute-start | bytes 221192 | tf_op jit(solution)/shard_map/ppermute | solution.py:24
  22.0 12.1 %copy-start.2 = (bf16[192,192]{1,0:T(8,128)(2,1)S(1)}, bf16[192,192]{1,0:T(8,128)(2,1)}, u32[]{:S(2)}) copy-start(bf16[192,192]{1,0:T(8,128)(2,1)} %param.10) | copy-start | bytes 221188
  22.0 41.9 %copy-start.3 = (bf16[96,384]{1,0:T(8,128)(2,1)S(1)}, bf16[96,384]{1,0:T(8,128)(2,1)}, u32[]{:S(2)}) copy-start(bf16[96,384]{1,0:T(8,128)(2,1)} %param.11) | copy-start | bytes 221188
  70.1 44.6 %copy-start.4 = (bf16[96,384]{1,0:T(8,128)(2,1)S(1)}, bf16[96,384]{1,0:T(8,128)(2,1)}, u32[]{:S(2)}) copy-start(bf16[96,384]{1,0:T(8,128)(2,1)} %param.12) | copy-start | bytes 221188
  121.9 6.2 %collective-permute-start.1 = (bf16[192,192]{1,0:T(8,128)(2,1)}, bf16[192,192]{1,0:T(8,128)(2,1)S(1)}, u32[]{:S(2)}, u32[]{:S(2)}) collective-permute-start(bf16[192,192]{1,0:T(8,128)(2,1)} %collective-permute-done), channel_id=1, source_target_pairs={{0,1},{1,2},{2,3},{3,4},{4,5},{5,6},{6,7},{7,0},{8,9},{9,10},{10,1... | collective-permute-start | bytes 221192 | tf_op jit(solution)/shard_map/ppermute | solution.py:24
  128.3 5.7 %collective-permute-start.2 = (bf16[192,192]{1,0:T(8,128)(2,1)S(1)}, bf16[192,192]{1,0:T(8,128)(2,1)}, u32[]{:S(2)}, u32[]{:S(2)}) collective-permute-start(bf16[192,192]{1,0:T(8,128)(2,1)S(1)} %collective-permute-done.1), channel_id=1, source_target_pairs={{0,1},{1,2},{2,3},{3,4},{4,5},{5,6},{6,7},{7,0},{8,9},{9,10},{10,1... | collective-permute-start | bytes 221192 | tf_op jit(solution)/shard_map/ppermute | solution.py:24
  134.9 6.5 %collective-permute-start.3 = (bf16[192,192]{1,0:T(8,128)(2,1)}, bf16[192,192]{1,0:T(8,128)(2,1)S(1)}, u32[]{:S(2)}, u32[]{:S(2)}) collective-permute-start(bf16[192,192]{1,0:T(8,128)(2,1)} %collective-permute-done.2), channel_id=1, source_target_pairs={{0,1},{1,2},{2,3},{3,4},{4,5},{5,6},{6,7},{7,0},{8,9},{9,10},{10,1... | collective-permute-start | bytes 221192 | tf_op jit(solution)/shard_map/ppermute | solution.py:24
  141.5 7.5 %collective-permute-start.4 = (bf16[192,192]{1,0:T(8,128)(2,1)S(1)}, bf16[192,192]{1,0:T(8,128)(2,1)}, u32[]{:S(2)}, u32[]{:S(2)}) collective-permute-start(bf16[192,192]{1,0:T(8,128)(2,1)S(1)} %collective-permute-done.3), channel_id=1, source_target_pairs={{0,1},{1,2},{2,3},{3,4},{4,5},{5,6},{6,7},{7,0},{8,9},{9,10},{10,1... | collective-permute-start | bytes 221192 | tf_op jit(solution)/shard_map/ppermute | solution.py:24
  150.0 7.6 %collective-permute-start.5 = (bf16[192,192]{1,0:T(8,128)(2,1)}, bf16[192,192]{1,0:T(8,128)(2,1)S(1)}, u32[]{:S(2)}, u32[]{:S(2)}) collective-permute-start(bf16[192,192]{1,0:T(8,128)(2,1)} %collective-permute-done.4), channel_id=1, source_target_pairs={{0,1},{1,2},{2,3},{3,4},{4,5},{5,6},{6,7},{7,0},{8,9},{9,10},{10,1... | collective-permute-start | bytes 221192 | tf_op jit(solution)/shard_map/ppermute | solution.py:24
  157.6 7.5 %collective-permute-start.6 = (bf16[192,192]{1,0:T(8,128)(2,1)S(1)}, bf16[192,192]{1,0:T(8,128)(2,1)}, u32[]{:S(2)}, u32[]{:S(2)}) collective-permute-start(bf16[192,192]{1,0:T(8,128)(2,1)S(1)} %collective-permute-done.5), channel_id=1, source_target_pairs={{0,1},{1,2},{2,3},{3,4},{4,5},{5,6},{6,7},{7,0},{8,9},{9,10},{10,1... | collective-permute-start | bytes 221192 | tf_op jit(solution)/shard_map/ppermute | solution.py:24
  267.0 78.8 %reduce-scatter.6.cloned.1.call-start = ((), (), s32[]{:S(2)}) async-start(), calls=%async_computation.4 | async-start | bytes 737280 | tf_op jit(solution)/shard_map/reduce_scatter | solution.py:109
  275.1 2.2 copy-start.1
  279.7 102.1 %reduce-scatter.10.cloned.1.call-start = ((), (), s32[]{:S(2)}) async-start(), calls=%async_computation.6 | async-start | bytes 1769472
  284.1 175.7 %all-reduce.2.cloned.1.call-start = ((), (), s32[]{:S(2)}) async-start(), calls=%async_computation.3 | async-start | bytes 393216 | tf_op jit(solution)/shard_map/psum | solution.py:95
Sparse Core Ops, SparseCore 0:
  267.1 21.4 reduce-scatter.7
  291.1 22.0 reduce-scatter.5
  316.6 65.1 reduce-scatter.9
Sparse Core Ops, SparseCore 1:
  332.7 127.0 all-reduce.1
